TPU v7x, 32 devices: a whole 2x2x4 slice. The times are simulated.
32 devices in a mesh: gx: 8 (over z, y), gy: 4 (over x, core).
Axes of the slice: x: 2, y: 2, z: 4, core: 2. Of those that a mesh axis runs over, the one named last changes fastest.
Arguments:
- output_one: bfloat16 [300, 12, 1024], P(None, 'gy', 'gx'), may hold values from -6 to 6
- output_two: bfloat16 [300, 12, 1024], P(None, 'gy', 'gx'), may hold values from -6 to 6
- cotan_one: bfloat16 [300, 12, 1024], P(None, 'gy', 'gx'), may hold values from -6 to 6
- cotan_two: bfloat16 [300, 12, 1024], P(None, 'gy', 'gx'), may hold values from -6 to 6
- wet_list: int32 [4, 8, 8, 48], P('gy', 'gx'), may hold values from -1 to 383, as said below
- depth_kernel: bfloat16 [300, 7, 7], replicated, may hold values from -0.875 to 0.875
- expand_weight: bfloat16 [300, 1200], replicated, may hold values from -0.375 to 0.375
- reduce_weight: bfloat16 [1200, 300], replicated, may hold values from -0.1875 to 0.1875
- level_expand: bfloat16 [4, 75, 300], replicated, may hold values from -0.75 to 0.75
- level_reduce: bfloat16 [4, 300, 75], replicated, may hold values from -0.375 to 0.375
Outputs:
- input_one: bfloat16 [300, 12, 1024], P(None, 'gy', 'gx')
- input_two: bfloat16 [300, 12, 1024], P(None, 'gy', 'gx')
- grad_input_one: bfloat16 [300, 12, 1024], P(None, 'gy', 'gx')
- grad_input_two: bfloat16 [300, 12, 1024], P(None, 'gy', 'gx')
- grad_kernel: float32 [300, 7, 7], replicated
- grad_expand: float32 [300, 1200], replicated
- grad_reduce: float32 [1200, 300], replicated
- grad_level_expand: float32 [4, 75, 300], replicated
- grad_level_reduce: float32 [4, 300, 75], replicated
Inputs may be any that keep to these rules, and one draw needn't show every extreme that they name: wet_list[j, i, p, s] is -1 or a cell index row * 128 + column inside the tile at gy index j and gx index i, listed for owner p of the same latitude row of tiles; the indices listed by one tile are distinct and are exactly its wet cells; a tile lists at most 48 cells for one owner, and one owner is listed at most 216 cells by all tiles of its row together.
All inputs are finite; a program needn't handle non-finite values.
Results may differ from a plain program's by a relative error of at most 0.0078.
Values may be sent and summed in bfloat16 or wider, within the bound.
A program may use at most 128 MiB of HBM per device.

v0:
```python
import math

import jax
import jax.numpy as jnp
from jax import lax
from jax.sharding import PartitionSpec as P

EPSILON = 1e-06


def with_halo(shard, sides, width):
    for axis, dim in sides:
        devices, length = (lax.axis_size(axis), shard.shape[dim])
        up = [(i, (i + 1) % devices) for i in range(devices)]
        down = [(j, i) for i, j in up]
        last = lax.slice_in_dim(shard, length - width, length, axis=dim)
        first = lax.slice_in_dim(shard, 0, width, axis=dim)
        before = lax.ppermute(last, axis, up)
        after = lax.ppermute(first, axis, down)
        shard = jnp.concatenate([before, shard, after], axis=dim)
    return shard


def swapped(shard, axis, stride):
    return lax.ppermute(shard, axis, [(i, i ^ 1 << stride) for i in range(lax.axis_size(axis))])


def gelu_slope(argument):
    normal_cdf = 0.5 * (1.0 + lax.erf(argument * 0.7071067811865476))
    return normal_cdf + argument * jnp.exp(-0.5 * argument * argument) * 0.3989422804014327


def level_branch(first_in, second, cot_first, cot_second, cell_mask, level_expand, level_reduce):
    groups, levels, expand_width = level_expand.shape
    column_count = first_in.shape[1]
    grouped = first_in.reshape(groups, levels, column_count)
    level_pre = jnp.einsum(
        "gls,gle->ges", grouped, level_expand, preferred_element_type=jnp.float32
    )
    active = jax.nn.gelu(level_pre, approximate=False).astype(jnp.bfloat16)
    mixed_out = jnp.einsum("ges,gel->gls", active, level_reduce, preferred_element_type=jnp.float32)
    mixed_out = mixed_out.reshape(groups * levels, column_count) * cell_mask[None, :]
    rebuilt = (second.astype(jnp.float32) - mixed_out).astype(jnp.bfloat16)
    upstream = (cot_second * cell_mask.astype(jnp.bfloat16)[None, :]).reshape(
        groups, levels, column_count
    )
    back_act = jnp.einsum(
        "gls,gel->ges", upstream, level_reduce, preferred_element_type=jnp.float32
    )
    back_pre = (back_act * gelu_slope(level_pre)).astype(jnp.bfloat16)
    back_in = jnp.einsum("ges,gle->gls", back_pre, level_expand, preferred_element_type=jnp.float32)
    total_one = (
        cot_first.astype(jnp.float32) + back_in.reshape(groups * levels, column_count)
    ).astype(jnp.bfloat16)
    grad_in = jnp.einsum("gls,ges->gle", grouped, back_pre, preferred_element_type=jnp.float32)
    grad_out = jnp.einsum("ges,gls->gel", active, upstream, preferred_element_type=jnp.float32)
    return (rebuilt, total_one, grad_in, grad_out)


def padded_rims(field_in):
    extended = with_halo(field_in, (("gx", 2), ("gy", 1)), 3)
    tile_rows = field_in.shape[1]
    at_south = lax.axis_index("gy") == 0
    at_north = lax.axis_index("gy") == lax.axis_size("gy") - 1
    row_ids = lax.broadcasted_iota(jnp.int32, (1, extended.shape[1], 1), 1)
    cut_rows = at_south & (row_ids < 3) | at_north & (row_ids >= tile_rows + 3)
    return jnp.where(cut_rows, jnp.zeros_like(extended), extended)


def mirrored(rim_rows):
    for bit_index in range(lax.axis_size("gx").bit_length() - 1):
        rim_rows = swapped(rim_rows, "gx", bit_index)
    return rim_rows


def folded_rims(field_in):
    tile_rows = field_in.shape[1]
    extended = padded_rims(field_in)
    partner = mirrored(extended[:, tile_rows : tile_rows + 3, :])
    upper_rows = partner[:, ::-1, ::-1]
    at_north = lax.axis_index("gy") == lax.axis_size("gy") - 1
    upper_rows = jnp.where(at_north, upper_rows, extended[:, tile_rows + 3 :, :])
    return jnp.concatenate([extended[:, : tile_rows + 3, :], upper_rows], axis=1)


def body(
    output_one,
    output_two,
    cotan_one,
    cotan_two,
    wet_list,
    depth_kernel,
    expand_weight,
    reduce_weight,
    level_expand,
    level_reduce,
):
    channels, tile_rows, tile_cols = output_one.shape
    tile_cells = tile_rows * tile_cols
    flat_one = output_one.reshape(channels, tile_cells)
    flat_two = output_two.reshape(channels, tile_cells)
    flat_cot_one = cotan_one.reshape(channels, tile_cells)
    flat_cot_two = cotan_two.reshape(channels, tile_cells)
    owner_count = wet_list.shape[2]
    slot_count = wet_list.shape[3]
    listing = wet_list.reshape(owner_count, slot_count)
    present = listing >= 0
    cell_index = jnp.where(present, listing, tile_cells).reshape(-1)
    wet_mask = jnp.zeros((tile_cells,), jnp.float32).at[cell_index].set(1.0, mode="drop")
    two_flat, total_flat, grad_level_in, grad_level_out = level_branch(
        flat_one, flat_two, flat_cot_one, flat_cot_two, wet_mask, level_expand, level_reduce
    )
    input_two = two_flat.reshape(channels, tile_rows, tile_cols)
    padded = folded_rims(input_two)
    wide_field = padded.astype(jnp.float32)
    kernel_wide = depth_kernel.astype(jnp.float32)
    spread = jnp.zeros((channels, tile_rows, tile_cols), jnp.float32)
    for row_tap in range(7):
        for col_tap in range(7):
            spread = (
                spread
                + kernel_wide[:, row_tap, col_tap][:, None, None]
                * wide_field[:, row_tap : row_tap + tile_rows, col_tap : col_tap + tile_cols]
            )
    spread = spread.reshape(channels, tile_cells)
    center = spread - jnp.mean(spread, axis=0, keepdims=True)
    rescale = lax.rsqrt(jnp.mean(center * center, axis=0, keepdims=True) + EPSILON)
    normal = center * rescale
    normal_half = normal.astype(jnp.bfloat16)
    contract_first = (((0,), (0,)), ((), ()))
    contract_last = (((1,), (1,)), ((), ()))
    contract_inner = (((1,), (0,)), ((), ()))
    hidden_pre = lax.dot_general(
        expand_weight, normal_half, contract_first, preferred_element_type=jnp.float32
    )
    hidden = jax.nn.gelu(hidden_pre, approximate=False).astype(jnp.bfloat16)
    update = lax.dot_general(
        reduce_weight, hidden, contract_first, preferred_element_type=jnp.float32
    )
    input_one = (flat_one.astype(jnp.float32) - update * wet_mask[None, :]).astype(jnp.bfloat16)
    upstream = total_flat * wet_mask.astype(jnp.bfloat16)[None, :]
    grad_reduce = lax.dot_general(
        hidden, upstream, contract_last, preferred_element_type=jnp.float32
    )
    back_hidden = lax.dot_general(
        reduce_weight, upstream, contract_inner, preferred_element_type=jnp.float32
    )
    back_pre = (back_hidden * gelu_slope(hidden_pre)).astype(jnp.bfloat16)
    grad_expand = lax.dot_general(
        normal_half, back_pre, contract_last, preferred_element_type=jnp.float32
    )
    back_normal = lax.dot_general(
        expand_weight, back_pre, contract_inner, preferred_element_type=jnp.float32
    )
    mean_back = jnp.mean(back_normal, axis=0, keepdims=True)
    mean_cross = jnp.mean(back_normal * normal, axis=0, keepdims=True)
    back_spread = (rescale * (back_normal - mean_back - normal * mean_cross)).astype(jnp.bfloat16)
    back_spread = back_spread.reshape(channels, tile_rows, tile_cols)
    back_field = back_spread.astype(jnp.float32)
    tap_rows = []
    for row_tap in range(7):
        tap_cols = []
        for col_tap in range(7):
            tap_cols.append(
                jnp.sum(
                    back_field
                    * wide_field[:, row_tap : row_tap + tile_rows, col_tap : col_tap + tile_cols],
                    axis=(1, 2),
                )
            )
        tap_rows.append(jnp.stack(tap_cols, axis=1))
    grad_kernel = jnp.stack(tap_rows, axis=1)
    back_padded = padded_rims(back_spread)
    back_wide = back_padded.astype(jnp.float32)
    main_part = jnp.zeros((channels, tile_rows, tile_cols), jnp.float32)
    for row_tap in range(7):
        for col_tap in range(7):
            main_part = (
                main_part
                + kernel_wide[:, row_tap, col_tap][:, None, None]
                * back_wide[
                    :, 6 - row_tap : 6 - row_tap + tile_rows, 6 - col_tap : 6 - col_tap + tile_cols
                ]
            )
    partner = mirrored(back_padded[:, tile_rows : tile_rows + 3, :])
    turned = partner[:, :, ::-1].astype(jnp.float32)
    pieces = []
    for fold_step in (3, 2, 1):
        row_total = jnp.zeros((channels, tile_cols), jnp.float32)
        for row_tap in range(3 + fold_step, min(6, 5 + fold_step) + 1):
            source_row = 5 + fold_step - row_tap
            for col_tap in range(7):
                row_total = (
                    row_total
                    + kernel_wide[:, row_tap, col_tap][:, None]
                    * turned[:, source_row, col_tap : col_tap + tile_cols]
                )
        pieces.append(row_total)
    fold_part = jnp.stack(pieces, axis=1)
    at_north = lax.axis_index("gy") == lax.axis_size("gy") - 1
    fold_part = jnp.where(at_north, fold_part, jnp.zeros_like(fold_part))
    through = main_part.at[:, tile_rows - 3 :, :].add(fold_part)
    grad_input_two = (cotan_two.astype(jnp.float32) + through).astype(jnp.bfloat16)
    summed = lax.psum(
        (grad_kernel, grad_expand, grad_reduce, grad_level_in, grad_level_out), ("gx", "gy")
    )
    factor = 1.0 / math.sqrt(tile_cells * lax.axis_size("gx") * lax.axis_size("gy"))
    return (
        input_one.reshape(channels, tile_rows, tile_cols),
        input_two,
        total_flat.reshape(channels, tile_rows, tile_cols),
        grad_input_two,
        summed[0] * factor,
        summed[1] * factor,
        summed[2] * factor,
        summed[3] * factor,
        summed[4] * factor,
    )


def solution(mesh):
    placed = (
        P(None, "gy", "gx"),
        P(None, "gy", "gx"),
        P(None, "gy", "gx"),
        P(None, "gy", "gx"),
        P("gy", "gx", None, None),
        P(),
        P(),
        P(),
        P(),
        P(),
    )
    return jax.shard_map(
        body,
        mesh=mesh,
        in_specs=placed,
        out_specs=(
            P(None, "gy", "gx"),
            P(None, "gy", "gx"),
            P(None, "gy", "gx"),
            P(None, "gy", "gx"),
            P(),
            P(),
            P(),
            P(),
            P(),
        ),
        check_vma=False,
    )
```

profile of v0, /device:TPU:0, one launch (start us, length us, event | category | flops | bytes accessed | tf_op | source)
XLA Modules:
  0.0 472.8 jit_solution(17439408598463731734)
XLA Ops:
  9.4 2.0 fusion.139
  11.4 4.2 fusion.4
  17.2 2.9 scatter_custom_fusion
  21.4 3.0 collective-permute-start
  24.4 3.0 collective-permute-start.1
  27.9 2.3 fusion.10
  33.5 4.3 collective-permute-done
  37.8 2.2 collective-permute-done.1
  40.0 1.8 pad_maximum_fusion
  50.6 2.1 copy.89
  52.9 2.1 copy.88
  55.1 4.5 maximum_select_fusion
  60.8 2.1 copy.90
  63.2 2.6 fusion.147
  65.8 6.4 %collective-permute-done.4 = bf16[300,3,134]{0,2,1:T(8,128)(2,1)S(1)} collective-permute-done((bf16[300,3,134]{0,2,1:T(8,128)(2,1)}, bf16[300,3,134]{0,2,1:T(8,128)(2,1)S(1)}, u32[]{:S(2)}, u32[]{:S(2)}) %collective-permute-start.4) | collective-permute-done | bytes 241232 | tf_op jit(solution)/shard_map/ppermute | solution.py:25
  72.2 2.7 collective-permute-start.5
  76.2 6.3 %collective-permute-done.5 = bf16[300,3,134]{0,2,1:T(8,128)(2,1)S(1)} collective-permute-done((bf16[300,3,134]{0,2,1:T(8,128)(2,1)S(1)}, bf16[300,3,134]{0,2,1:T(8,128)(2,1)S(1)}, u32[]{:S(2)}, u32[]{:S(2)}) %collective-permute-start.5) | collective-permute-done | bytes 241232 | tf_op jit(solution)/shard_map/ppermute | solution.py:25
  82.5 2.0 collective-permute-start.6
  86.4 12.0 %collective-permute-done.6 = bf16[300,3,134]{0,2,1:T(8,128)(2,1)} collective-permute-done((bf16[300,3,134]{0,2,1:T(8,128)(2,1)S(1)}, bf16[300,3,134]{0,2,1:T(8,128)(2,1)}, u32[]{:S(2)}, u32[]{:S(2)}) %collective-permute-start.6) | collective-permute-done | bytes 241232 | tf_op jit(solution)/shard_map/ppermute | solution.py:25
  98.4 2.1 copy.91
  100.6 5.4 %reverse = bf16[300,3,256]{2,1,0:T(4,128)(2,1)} reverse(bf16[300,3,256]{2,1,0:T(4,128)(2,1)} %bitcast.91), dimensions={1,2} | reverse | bytes 921600
  105.9 2.1 slice_select_fusion
  109.8 36.7 %fusion.167 = (f32[3,128]{1,0:T(4,128)S(1)}, f32[300,3,128]{2,1,0:T(4,128)S(1)}) fusion(f32[300,9,134]{2,1,0:T(8,128)S(1)} %maximum_convert_fusion, f32[300]{0:T(512)S(1)} %get-tuple-element.117, f32[300]{0:T(512)S(1)} %get-tuple-element.118, f32[300]{0:T(512)S(1)} %get-tuple-element.119, f32[300]{0:T(512)S(1)} %copy-done.35, f32[300]{0:T(512)S(1)} %copy-done.37, ...), kind=kLoop, calls=%fused_computation.387 | loop fusion | flops 11289216 | bytes 23100336 | tf_op jit(solution)/shard_map/reduce_sum | solution.py:126
  147.1 4.4 fusion.19
  154.3 31.5 %fusion.80 = (f32[300]{0:T(512)S(1)}, f32[300]{0:T(512)S(1)}, f32[300]{0:T(512)S(1)}, f32[300]{0:T(512)S(1)}, f32[300]{0:T(512)S(1)}, /*index=5*/f32[300]{0:T(51...) fusion(bf16[300,3,128]{2,1,0:T(4,128)(2,1)S(1)} %reshape.526, ...), kind=kLoop, calls=%fused_computation.165 | loop fusion | flops 3106500 | bytes 6236400 | tf_op jit(solution)/shard_map/reduce_sum | solution.py:165
  185.9 34.6 %fusion.82 = (f32[300]{0:T(512)S(1)}, f32[300]{0:T(512)S(1)}, f32[300]{0:T(512)S(1)}, f32[300]{0:T(512)S(1)}, f32[300]{0:T(512)S(1)}, /*index=5*/f32[300]{0:T(51...) fusion(bf16[300,3,128]{2,1,0:T(4,128)(2,1)S(1)} %reshape.526, ...), kind=kLoop, calls=%fused_computation.167 | loop fusion | flops 4257000 | bytes 8546400 | tf_op jit(solution)/shard_map/reduce_sum | solution.py:165
  220.4 35.5 %fusion.81 = (f32[300]{0:T(512)S(1)}, f32[300]{0:T(512)S(1)}, f32[300]{0:T(512)S(1)}, f32[300]{0:T(512)S(1)}, f32[300]{0:T(512)S(1)}, /*index=5*/f32[300]{0:T(51...) fusion(bf16[300,3,128]{2,1,0:T(4,128)(2,1)S(1)} %reshape.526, ...), kind=kLoop, calls=%fused_computation.166 | loop fusion | flops 4257000 | bytes 8546400 | tf_op jit(solution)/shard_map/reduce_sum | solution.py:165
  256.0 1.8 fusion.159
  258.7 1.7 fusion.170
  261.1 1.6 collective-permute-start.7
  262.7 3.4 collective-permute-start.8
  266.3 9.1 %collective-permute-done.7 = bf16[300,3,3]{2,1,0:T(4,128)(2,1)S(1)} collective-permute-done((bf16[300,3,3]{2,1,0:T(4,128)(2,1)}, bf16[300,3,3]{2,1,0:T(4,128)(2,1)S(1)}, u32[]{:S(2)}, u32[]{:S(2)}) %collective-permute-start.7) | collective-permute-done | bytes 5432 | tf_op jit(solution)/shard_map/ppermute | solution.py:18
  275.4 2.1 collective-permute-done.8
  279.7 6.6 %collective-permute-done.10 = bf16[300,3,134]{0,2,1:T(8,128)(2,1)S(1)} collective-permute-done((bf16[300,3,134]{0,2,1:T(8,128)(2,1)S(1)}, bf16[300,3,134]{0,2,1:T(8,128)(2,1)S(1)}, u32[]{:S(2)}, u32[]{:S(2)}) %collective-permute-start.10) | collective-permute-done | bytes 241232 | tf_op jit(solution)/shard_map/ppermute | solution.py:19
  286.7 2.4 collective-permute-done.9
  289.6 4.8 %fusion.166 = (f32[300,9,134]{2,1,0:T(8,128)}, bf16[300,9,134]{2,1,0:T(8,128)(2,1)S(1)}) fusion(bf16[300,3,134]{2,1,0:T(4,128)(2,1)S(1)} %copy.100, bf16[300,3,3]{2,1,0:T(4,128)(2,1)S(1)} %collective-permute-done.8, bf16[300,3,128]{2,1,0:T(4,128)(2,1)S(1)} %reshape.526, bf16[300,3,3]{2,1,0:T(4,128)(2,1)S(1)} %collective-permute-done.7, ...), kind=kLoop, calls=%fused_computation.386 | loop fusion | flops 4341600 | bytes 2894409 | tf_op jit(solution)/shard_map/convert_element_type | solution.py:174
  295.4 9.6 %collective-permute-done.11 = bf16[300,3,134]{0,2,1:T(8,128)(2,1)S(1)} collective-permute-done((bf16[300,3,134]{0,2,1:T(8,128)(2,1)S(1)}, bf16[300,3,134]{0,2,1:T(8,128)(2,1)S(1)}, u32[]{:S(2)}, u32[]{:S(2)}) %collective-permute-start.11) | collective-permute-done | bytes 241232 | tf_op jit(solution)/shard_map/ppermute | solution.py:25
  306.3 9.0 %collective-permute-done.12 = bf16[300,3,134]{0,2,1:T(8,128)(2,1)S(1)} collective-permute-done((bf16[300,3,134]{0,2,1:T(8,128)(2,1)S(1)}, bf16[300,3,134]{0,2,1:T(8,128)(2,1)S(1)}, u32[]{:S(2)}, u32[]{:S(2)}) %collective-permute-start.12) | collective-permute-done | bytes 241232 | tf_op jit(solution)/shard_map/ppermute | solution.py:25
  315.3 2.3 collective-permute-start.13
  317.6 41.8 %psum.35 = f32[300,7,7]{0,2,1:T(8,128)S(1)} all-reduce(f32[300,7,7]{0,2,1:T(8,128)S(1)} %constant_dynamic-update-slice_fusion), channel_id=1, replica_groups=mesh['gx'=8,'gy'=4] {'gx','gy'}, use_global_device_ids=true, to_apply=%region_54.55 | all-reduce | flops 14700 | bytes 117600 | tf_op jit(solution)/shard_map/psum | solution.py:204
  360.7 3.1 reverse.1
  364.5 14.1 %fusion.150 = f32[300,1,128]{2,1,0:T(1,128)S(1)} fusion(f32[300,3,134]{2,1,0:T(4,128)S(1)} %slice_convert_fusion, f32[300]{0:T(512)S(1)} %copy-done.65, f32[300]{0:T(512)S(1)} %copy-done.67, f32[300]{0:T(512)S(1)} %copy-done.69, f32[300]{0:T(512)S(1)} %copy-done.71, f32[300]{0:T(512)S(1)} %copy-done.59, f32[300]{0:T(512)S(1)} %copy-done.61, ...), kind=kLoop, calls=%fused_computation.300 | loop fusion | flops 1574400 | bytes 3404400 | tf_op jit(solution)/shard_map/add | solution.py:194
  378.8 9.3 %multiply_add_fusion.1 = f32[300,1,128]{2,1,0:T(1,128)S(1)} fusion(f32[300,3,134]{2,1,0:T(4,128)S(1)} %slice_convert_fusion, f32[300]{0:T(512)S(1)} %copy-done.44, f32[300]{0:T(512)S(1)} %copy-done.46, f32[300]{0:T(512)S(1)} %copy-done.48, f32[300]{0:T(512)S(1)} %copy-done.50, f32[300]{0:T(512)S(1)} %copy-done.52, f32[300]{0:T(512)S(1)} %copy-done.54, ...), kind=kLoop, calls=%fused_computation.313 | loop fusion | flops 1036800 | bytes 2320800 | tf_op jit(solution)/shard_map/add | solution.py:194
  388.1 4.6 multiply_add_fusion.2
  392.9 37.2 %fusion.86 = bf16[300,3,128]{2,1,0:T(4,128)(2,1)S(1)} fusion(f32[300,9,134]{2,1,0:T(8,128)S(1)} %bitcast.83, f32[300,1,128]{2,1,0:T(1,128)S(1)} %fusion.150, f32[300,1,128]{2,1,0:T(1,128)S(1)} %multiply_add_fusion.1, f32[300,1,128]{2,1,0:T(1,128)S(1)} %multiply_add_fusion.2, f32[300]{0:T(512)S(1)} %copy-done.30, f32[300]{0:T(512)S(1)} %copy-done.32, ...), kind=kLoop, calls=%fused_computation.172 | loop fusion | flops 11980800 | bytes 23559600 | tf_op jit(solution)/shard_map/convert_element_type | solution.py:203
  430.8 28.6 %all-reduce.3.cloned.1.call-done = (f32[300,1200]{1,0:T(8,128)}, f32[1200,300]{0,1:T(8,128)}, f32[4,75,300]{2,1,0:T(8,128)}, f32[4,300,75]{1,2,0:T(8,128)}) async-done(((f32[300,1200]{1,0:T(8,128)}, f32[1200,300]{0,1:T(8,128)}, f32[4,75,300]{2,1,0:T(8,128)}, f32[4,300,75]{1,2,0:T(8,128)}), (f32[300,1200]{1,0:T(8,128)}, f32[1200,300]{0,1:T(8,128)}, f32[4,75,300]{2,1,0:T(8,128)}, ...) | async-done | bytes 3600016 | tf_op jit(solution)/shard_map/psum | solution.py:204
  459.5 2.8 broadcast_multiply_fusion.1
  464.2 1.3 broadcast_multiply_fusion
  (379 shorter events, 37.6 us)
Async XLA Ops:
  7.2 139.9 %copy-start = (bf16[300,1200]{1,0:T(8,128)(2,1)S(1)}, bf16[300,1200]{1,0:T(8,128)(2,1)}, u32[]{:S(2)}) copy-start(bf16[300,1200]{1,0:T(8,128)(2,1)} %param.20) | copy-start | bytes 2160004
  7.2 452.3 %all-reduce.3.cloned.1.call-start = ((), (), s32[]{:S(2)}) async-start(), calls=%async_computation | async-start | bytes 8192000 | tf_op jit(solution)/shard_map/psum | solution.py:204
  16.9 10.5 %copy-start.16 = (bf16[300,3,128]{2,0,1:T(8,128)(2,1)S(1)}, bf16[300,3,128]{2,0,1:T(8,128)(2,1)}, u32[]{:S(2)}) copy-start(bf16[300,3,128]{2,0,1:T(8,128)(2,1)} %param.17) | copy-start | bytes 691204
  17.1 10.6 %copy-start.18 = (bf16[300,3,128]{2,0,1:T(8,128)(2,1)S(1)}, bf16[300,3,128]{2,0,1:T(8,128)(2,1)}, u32[]{:S(2)}) copy-start(bf16[300,3,128]{2,0,1:T(8,128)(2,1)} %param.16) | copy-start | bytes 691204
  21.4 16.4 %collective-permute-start = (bf16[300,3,3]{2,1,0:T(4,128)(2,1)}, bf16[300,3,3]{2,1,0:T(4,128)(2,1)S(1)}, u32[]{:S(2)}, u32[]{:S(2)}) collective-permute-start(bf16[300,3,3]{2,1,0:T(4,128)(2,1)} %get-tuple-element.175), channel_id=1, source_target_pairs={{0,4},{4,8},{8,12},{12,16},{16,20},{20,24},{24,28},{28,0},{1,5},{5... | collective-permute-start | bytes 16208 | tf_op jit(solution)/shard_map/ppermute | solution.py:18
  24.4 15.6 %collective-permute-start.1 = (bf16[300,3,3]{2,1,0:T(4,128)(2,1)}, bf16[300,3,3]{2,1,0:T(4,128)(2,1)}, u32[]{:S(2)}, u32[]{:S(2)}) collective-permute-start(bf16[300,3,3]{2,1,0:T(4,128)(2,1)} %get-tuple-element.176), channel_id=1, source_target_pairs={{4,0},{8,4},{12,8},{16,12},{20,16},{24,20},{28,24},{0,28},{5,1},{9... | collective-permute-start | bytes 16208 | tf_op jit(solution)/shard_map/ppermute | solution.py:19
  42.9 7.8 %collective-permute-start.3 = (bf16[300,3,134]{0,2,1:T(8,128)(2,1)}, bf16[300,3,134]{0,2,1:T(8,128)(2,1)}, u32[]{:S(2)}, u32[]{:S(2)}) collective-permute-start(bf16[300,3,134]{0,2,1:T(8,128)(2,1)} %copy.86), channel_id=1, source_target_pairs={{1,0},{2,1},{3,2},{0,3},{5,4},{6,5},{7,6},{4,7},{9,8},{10,9},{11,1... | collective-permute-start | bytes 723608 | tf_op jit(solution)/shard_map/ppermute | solution.py:19
  42.9 10.1 %collective-permute-start.2 = (bf16[300,3,134]{0,2,1:T(8,128)(2,1)}, bf16[300,3,134]{0,2,1:T(8,128)(2,1)}, u32[]{:S(2)}, u32[]{:S(2)}) collective-permute-start(bf16[300,3,134]{0,2,1:T(8,128)(2,1)} %copy.86), channel_id=1, source_target_pairs={{0,1},{1,2},{2,3},{3,0},{4,5},{5,6},{6,7},{7,4},{8,9},{9,10},{10,1... | collective-permute-start | bytes 723608 | tf_op jit(solution)/shard_map/ppermute | solution.py:18
  50.6 58.8 %copy-start.29 = (f32[300]{0:T(512)}, f32[300]{0:T(512)S(1)}, u32[]{:S(2)}) copy-start(f32[300]{0:T(512)S(1)} %get-tuple-element.117) | copy-start | bytes 3604
  50.6 58.8 %copy-start.31 = (f32[300]{0:T(512)}, f32[300]{0:T(512)S(1)}, u32[]{:S(2)}) copy-start(f32[300]{0:T(512)S(1)} %get-tuple-element.118) | copy-start | bytes 3604
  50.6 58.8 %copy-start.33 = (f32[300]{0:T(512)}, f32[300]{0:T(512)S(1)}, u32[]{:S(2)}) copy-start(f32[300]{0:T(512)S(1)} %get-tuple-element.119) | copy-start | bytes 3604
  59.6 15.3 %copy-start.14 = (bf16[4,75,384]{2,1,0:T(8,128)(2,1)S(1)}, bf16[4,75,384]{2,1,0:T(8,128)(2,1)}, u32[]{:S(2)}) copy-start(bf16[4,75,384]{2,1,0:T(8,128)(2,1)} %copy-done.13) | copy-start | bytes 691204
  62.9 12.1 %copy-start.6 = (bf16[4,300,384]{2,1,0:T(8,128)(2,1)S(1)}, bf16[4,300,384]{2,1,0:T(8,128)(2,1)}, u32[]{:S(2)}) copy-start(bf16[4,300,384]{2,1,0:T(8,128)(2,1)} %copy-done.5) | copy-start | bytes 2764804
  62.9 21.7 %copy-start.8 = (f32[300,384]{1,0:T(8,128)S(1)}, f32[300,384]{1,0:T(8,128)}, u32[]{:S(2)}) copy-start(f32[300,384]{1,0:T(8,128)} %reshape.525) | copy-start | bytes 1382404
  62.9 21.7 %copy-start.9 = (f32[38,8,3,128]{3,1,2,0:T(8,128)S(1)}, f32[38,8,3,128]{3,1,2,0:T(8,128)}, u32[]{:S(2)}) copy-start(f32[38,8,3,128]{3,1,2,0:T(8,128)} %copy.111) | copy-start | bytes 1400836
  62.9 9.4 %collective-permute-start.4 = (bf16[300,3,134]{0,2,1:T(8,128)(2,1)}, bf16[300,3,134]{0,2,1:T(8,128)(2,1)S(1)}, u32[]{:S(2)}, u32[]{:S(2)}) collective-permute-start(bf16[300,3,134]{0,2,1:T(8,128)(2,1)} %copy.90), channel_id=1, source_target_pairs={{0,4},{4,0},{8,12},{12,8},{16,20},{20,16},{24,28},{28,24},{1,5},{5... | collective-permute-start | bytes 723608 | tf_op jit(solution)/shard_map/ppermute | solution.py:25
  72.2 10.3 %collective-permute-start.5 = (bf16[300,3,134]{0,2,1:T(8,128)(2,1)S(1)}, bf16[300,3,134]{0,2,1:T(8,128)(2,1)S(1)}, u32[]{:S(2)}, u32[]{:S(2)}) collective-permute-start(bf16[300,3,134]{0,2,1:T(8,128)(2,1)S(1)} %collective-permute-done.4), channel_id=1, source_target_pairs={{0,8},{4,12},{8,0},{12,4},{16,24},{20,28},{24,16},{28,20},{1,9},{5... | collective-permute-start | bytes 723608 | tf_op jit(solution)/shard_map/ppermute | solution.py:25
  82.5 15.9 %collective-permute-start.6 = (bf16[300,3,134]{0,2,1:T(8,128)(2,1)S(1)}, bf16[300,3,134]{0,2,1:T(8,128)(2,1)}, u32[]{:S(2)}, u32[]{:S(2)}) collective-permute-start(bf16[300,3,134]{0,2,1:T(8,128)(2,1)S(1)} %collective-permute-done.5), channel_id=1, source_target_pairs={{0,16},{4,20},{8,24},{12,28},{16,0},{20,4},{24,8},{28,12},{1,17},{... | collective-permute-start | bytes 723608 | tf_op jit(solution)/shard_map/ppermute | solution.py:25
  109.4 37.2 %copy-start.2 = (f32[300,9,134]{2,1,0:T(8,128)}, f32[300,9,134]{2,1,0:T(8,128)S(1)}, u32[]{:S(2)}) copy-start(f32[300,9,134]{2,1,0:T(8,128)S(1)} %maximum_convert_fusion) | copy-start | bytes 4341604
  220.4 35.5 %copy-start.75 = (f32[384]{0:T(512)S(1)}, f32[384]{0:T(512)}, u32[]{:S(2)}) copy-start(f32[384]{0:T(512)} %copy-done.74) | copy-start | bytes 4612
  220.4 35.5 %copy-start.77 = (f32[384]{0:T(512)S(1)}, f32[384]{0:T(512)}, u32[]{:S(2)}) copy-start(f32[384]{0:T(512)} %copy-done.76) | copy-start | bytes 4612
  261.1 14.3 %collective-permute-start.7 = (bf16[300,3,3]{2,1,0:T(4,128)(2,1)}, bf16[300,3,3]{2,1,0:T(4,128)(2,1)S(1)}, u32[]{:S(2)}, u32[]{:S(2)}) collective-permute-start(bf16[300,3,3]{2,1,0:T(4,128)(2,1)} %get-tuple-element.173), channel_id=1, source_target_pairs={{0,4},{4,8},{8,12},{12,16},{16,20},{20,24},{24,28},{28,0},{1,5},{5... | collective-permute-start | bytes 16208 | tf_op jit(solution)/shard_map/ppermute | solution.py:18
  262.7 14.8 %collective-permute-start.8 = (bf16[300,3,3]{2,1,0:T(4,128)(2,1)S(1)}, bf16[300,3,3]{2,1,0:T(4,128)(2,1)S(1)}, u32[]{:S(2)}, u32[]{:S(2)}) collective-permute-start(bf16[300,3,3]{2,1,0:T(4,128)(2,1)S(1)} %get-tuple-element.174), channel_id=1, source_target_pairs={{4,0},{8,4},{12,8},{16,12},{20,16},{24,20},{28,24},{0,28},{5,1},{9... | collective-permute-start | bytes 16208 | tf_op jit(solution)/shard_map/ppermute | solution.py:19
  266.3 23.3 %copy-start.116 = (pred[9]{0:T(512)(128)(4,1)S(1)}, pred[9]{0:T(512)(128)(4,1)}, u32[]{:S(2)}) copy-start(pred[9]{0:T(512)(128)(4,1)} %and_or_fusion) | copy-start | bytes 31
  278.8 7.6 %collective-permute-start.10 = (bf16[300,3,134]{0,2,1:T(8,128)(2,1)S(1)}, bf16[300,3,134]{0,2,1:T(8,128)(2,1)S(1)}, u32[]{:S(2)}, u32[]{:S(2)}) collective-permute-start(bf16[300,3,134]{0,2,1:T(8,128)(2,1)S(1)} %copy.97), channel_id=1, source_target_pairs={{1,0},{2,1},{3,2},{0,3},{5,4},{6,5},{7,6},{4,7},{9,8},{10,9},{11,1... | collective-permute-start | bytes 723608 | tf_op jit(solution)/shard_map/ppermute | solution.py:19
  279.5 9.7 %collective-permute-start.9 = (bf16[300,3,134]{0,2,1:T(8,128)(2,1)S(1)}, bf16[300,3,134]{0,2,1:T(8,128)(2,1)S(1)}, u32[]{:S(2)}, u32[]{:S(2)}) collective-permute-start(bf16[300,3,134]{0,2,1:T(8,128)(2,1)S(1)} %copy.97), channel_id=1, source_target_pairs={{0,1},{1,2},{2,3},{3,0},{4,5},{5,6},{6,7},{7,4},{8,9},{9,10},{10,1... | collective-permute-start | bytes 723608 | tf_op jit(solution)/shard_map/ppermute | solution.py:18
  295.1 9.9 %collective-permute-start.11 = (bf16[300,3,134]{0,2,1:T(8,128)(2,1)S(1)}, bf16[300,3,134]{0,2,1:T(8,128)(2,1)S(1)}, u32[]{:S(2)}, u32[]{:S(2)}) collective-permute-start(bf16[300,3,134]{0,2,1:T(8,128)(2,1)S(1)} %copy.101), channel_id=1, source_target_pairs={{0,4},{4,0},{8,12},{12,8},{16,20},{20,16},{24,28},{28,24},{1,5},{5... | collective-permute-start | bytes 723608 | tf_op jit(solution)/shard_map/ppermute | solution.py:25
  305.0 10.3 %collective-permute-start.12 = (bf16[300,3,134]{0,2,1:T(8,128)(2,1)S(1)}, bf16[300,3,134]{0,2,1:T(8,128)(2,1)S(1)}, u32[]{:S(2)}, u32[]{:S(2)}) collective-permute-start(bf16[300,3,134]{0,2,1:T(8,128)(2,1)S(1)} %collective-permute-done.11), channel_id=1, source_target_pairs={{0,8},{4,12},{8,0},{12,4},{16,24},{20,28},{24,16},{28,20},{1,9},{5... | collective-permute-start | bytes 723608 | tf_op jit(solution)/shard_map/ppermute | solution.py:25
  306.2 86.5 %slice-start = ((s8[4915200]{0:T(1024)(128)(4,1)}), s8[720896]{0:T(1024)(128)(4,1)S(1)}, s32[]{:S(2)}) async-start(s8[4915200]{0:T(1024)(128)(4,1)} %bitcast.82), calls=%async_computation.1 | async-start | bytes 1441792
  315.3 45.0 %collective-permute-start.13 = (bf16[300,3,134]{0,2,1:T(8,128)(2,1)S(1)}, bf16[300,3,134]{0,2,1:T(8,128)(2,1)S(1)}, u32[]{:S(2)}, u32[]{:S(2)}) collective-permute-start(bf16[300,3,134]{0,2,1:T(8,128)(2,1)S(1)} %collective-permute-done.12), channel_id=1, source_target_pairs={{0,16},{4,20},{8,24},{12,28},{16,0},{20,4},{24,8},{28,12},{1,17},{... | collective-permute-start | bytes 723608 | tf_op jit(solution)/shard_map/ppermute | solution.py:25
  363.8 28.9 %slice-start.1 = ((s8[4915200]{0:T(1024)(128)(4,1)}), s8[4194304]{0:T(1024)(128)(4,1)S(1)}, s32[]{:S(2)}) async-start(s8[4915200]{0:T(1024)(128)(4,1)} %bitcast.82), calls=%async_computation.2 | async-start | bytes 8388608
  378.6 14.1 %copy-start.17 = (bf16[300,3,128]{2,0,1:T(8,128)(2,1)S(1)}, bf16[300,3,128]{2,0,1:T(8,128)(2,1)}, u32[]{:S(2)}) copy-start(bf16[300,3,128]{2,0,1:T(8,128)(2,1)} %param.17) | copy-start | bytes 691204
  378.6 14.1 %copy-start.79 = (f32[300]{0:T(512)S(1)}, f32[300]{0:T(512)}, u32[]{:S(2)}) copy-start(f32[300]{0:T(512)} %get-tuple-element.154) | copy-start | bytes 3604
  378.6 14.1 %copy-start.81 = (f32[300]{0:T(512)S(1)}, f32[300]{0:T(512)}, u32[]{:S(2)}) copy-start(f32[300]{0:T(512)} %get-tuple-element.155) | copy-start | bytes 3604
  378.6 14.1 %copy-start.83 = (f32[300]{0:T(512)S(1)}, f32[300]{0:T(512)}, u32[]{:S(2)}) copy-start(f32[300]{0:T(512)} %get-tuple-element.156) | copy-start | bytes 3604
  378.7 14.1 %copy-start.85 = (f32[300]{0:T(512)S(1)}, f32[300]{0:T(512)}, u32[]{:S(2)}) copy-start(f32[300]{0:T(512)} %get-tuple-element.157) | copy-start | bytes 3604
  378.7 14.1 %copy-start.87 = (f32[300]{0:T(512)S(1)}, f32[300]{0:T(512)}, u32[]{:S(2)}) copy-start(f32[300]{0:T(512)} %get-tuple-element.158) | copy-start | bytes 3604
  378.7 14.1 %copy-start.89 = (f32[300]{0:T(512)S(1)}, f32[300]{0:T(512)}, u32[]{:S(2)}) copy-start(f32[300]{0:T(512)} %get-tuple-element.159) | copy-start | bytes 3604
  378.7 14.1 %copy-start.91 = (f32[300]{0:T(512)S(1)}, f32[300]{0:T(512)}, u32[]{:S(2)}) copy-start(f32[300]{0:T(512)} %get-tuple-element.160) | copy-start | bytes 3604
  378.7 14.1 %copy-start.93 = (f32[300]{0:T(512)S(1)}, f32[300]{0:T(512)}, u32[]{:S(2)}) copy-start(f32[300]{0:T(512)} %get-tuple-element.161) | copy-start | bytes 3604
  378.7 14.1 %copy-start.95 = (f32[300]{0:T(512)S(1)}, f32[300]{0:T(512)}, u32[]{:S(2)}) copy-start(f32[300]{0:T(512)} %get-tuple-element.162) | copy-start | bytes 3604
  378.7 14.1 %copy-start.97 = (f32[300]{0:T(512)S(1)}, f32[300]{0:T(512)}, u32[]{:S(2)}) copy-start(f32[300]{0:T(512)} %get-tuple-element.163) | copy-start | bytes 3604
  378.7 14.1 %copy-start.99 = (f32[300]{0:T(512)S(1)}, f32[300]{0:T(512)}, u32[]{:S(2)}) copy-start(f32[300]{0:T(512)} %get-tuple-element.164) | copy-start | bytes 3604
  378.7 14.1 %copy-start.101 = (f32[300]{0:T(512)S(1)}, f32[300]{0:T(512)}, u32[]{:S(2)}) copy-start(f32[300]{0:T(512)} %get-tuple-element.135) | copy-start | bytes 3604
  378.7 14.1 %copy-start.103 = (f32[300]{0:T(512)S(1)}, f32[300]{0:T(512)}, u32[]{:S(2)}) copy-start(f32[300]{0:T(512)} %get-tuple-element.139) | copy-start | bytes 3604
  378.8 14.1 %copy-start.105 = (f32[300]{0:T(512)S(1)}, f32[300]{0:T(512)}, u32[]{:S(2)}) copy-start(f32[300]{0:T(512)} %get-tuple-element.140) | copy-start | bytes 3604
  378.8 14.1 %copy-start.107 = (f32[300]{0:T(512)S(1)}, f32[300]{0:T(512)}, u32[]{:S(2)}) copy-start(f32[300]{0:T(512)} %get-tuple-element.141) | copy-start | bytes 3604
  378.8 14.1 %copy-start.109 = (f32[300]{0:T(512)S(1)}, f32[300]{0:T(512)}, u32[]{:S(2)}) copy-start(f32[300]{0:T(512)} %get-tuple-element.142) | copy-start | bytes 3604
  (86 other events, 250.1 us)
Sparse Core Ops, SparseCore 0:
  306.4 153.0 all-reduce.2
where the time goes:
time: 480 us; the launch traced here: 473 us
  other arithmetic  232 us (48%)
  waiting for transfers between devices  98.9 us (21%)
  local copies, waits for them, and re-layouts  44 us (9%)
  blocking collectives  41.8 us (9%)
  starting transfers between devices  20.4 us (4%)
  matrix products  19.1 us (4%)
  between operations  16.9 us (4%)
    reduce_sum x3, other arithmetic, body(): jnp.sum(back_field * wide_field[:, row_tap:row_tap + tile_rows, col_tap:c...  102 us
    ppermute x6, waiting for transfers between devices, swapped(): lax.ppermute(shard, axis, [(i, i ^ 1 << stride) for i in range(lax.axis_s...  43.3 us
    psum x1, blocking collectives, body(): lax.psum((grad_kernel, grad_expand, grad_reduce, grad_level_in, grad_leve...  41.8 us
    convert_element_type x1, other arithmetic, body(): (cotan_two.astype(jnp.float32) + through).astype(jnp.bfloat16)  37.2 us
    reduce_sum x1, other arithmetic, body(): center = spread - jnp.mean(spread, axis=0, keepdims=True)  36.7 us
    psum x1, waiting for transfers between devices, body(): lax.psum((grad_kernel, grad_expand, grad_reduce, grad_level_in, grad_leve...  28.6 us
    add x3, other arithmetic, body(): row_total + kernel_wide[:, row_tap, col_tap][:, None] * turned[:, source_...  28 us
    unnamed x260, local copies, waits for them, and re-layouts  18.8 us
  transfers between devices with their start and end apart: 15, of which 13 were waited for; matrix products, arithmetic and copies ran while one was open for 19% of the time, Pallas kernels for 0%

commit v1 on v0

v1 whole, which is shorter than its diff:
```python
import functools
import math

import jax
import jax.numpy as jnp
import numpy as np
from jax import lax
from jax.experimental import pallas as pl
from jax.experimental.pallas import tpu as pltpu
from jax.sharding import PartitionSpec as P

EPSILON = 1e-06
MESH = pl.DeviceIdType.MESH
F32 = jnp.float32
BF16 = jnp.bfloat16
REACH = 3
TAPS = 7
EDGE_ROWS = 16
WEST, EAST, NORTH_WEST, NORTH_EAST, SOUTH_WEST, SOUTH_EAST = range(6)


def dot(a, b, ca, cb):
    return lax.dot_general(a, b, (((ca,), (cb,)), ((), ())), preferred_element_type=F32)


def activate(pre_ref, back_ref, act_ref, bp_ref):
    def step(i, carry):
        rows = pl.ds(pl.multiple_of(i * 16, 16), 16)
        t = pre_ref[rows, :]
        cdf = 0.5 * (1.0 + lax.erf(t * 0.7071067811865476))
        act_ref[rows, :] = (t * cdf).astype(BF16)
        slope = cdf + t * jnp.exp(-0.5 * t * t) * 0.3989422804014327
        bp_ref[rows, :] = (back_ref[rows, :] * slope).astype(BF16)
        return carry

    lax.fori_loop(0, pre_ref.shape[0] // 16, step, 0)


def level_kernel(
    factor, slot, one, two, cot_one, cot_two, listing, le, lr, pick_left, pick_right,
    two_out, total_out, left_out, right_out, mask_out, gle, glr,
    a, b, c, d, pre, back, act, bp,
):
    groups, levels, width = le.shape
    channels, cells = one.shape
    entries = listing[...]
    cell_ids = lax.broadcasted_iota(jnp.int32, (entries.shape[0], cells), 1)
    hit = jnp.where(entries == cell_ids, 1.0, 0.0)
    mask = jnp.max(hit, axis=0, keepdims=True)
    mask_out[...] = jnp.broadcast_to(mask, mask_out.shape)
    a[...] = one[...].astype(F32)
    b[...] = cot_two[...].astype(F32) * mask
    for v in range(groups):
        g = a[v * levels : (v + 1) * levels, :].astype(BF16)
        u = b[v * levels : (v + 1) * levels, :].astype(BF16)
        pre[v * slot : v * slot + width, :] = dot(le[v], g, 0, 0)
        back[v * slot : v * slot + width, :] = dot(lr[v], u, 1, 0)
    activate(pre, back, act, bp)
    for v in range(groups):
        g = a[v * levels : (v + 1) * levels, :].astype(BF16)
        u = b[v * levels : (v + 1) * levels, :].astype(BF16)
        act_v = act[v * slot : v * slot + width, :]
        bp_v = bp[v * slot : v * slot + width, :]
        c[v * levels : (v + 1) * levels, :] = dot(lr[v], act_v, 0, 0)
        d[v * levels : (v + 1) * levels, :] = dot(le[v], bp_v, 1, 0)
        gle[v] = (dot(g, bp_v, 1, 1) * factor).astype(BF16)
        glr[v] = (dot(act_v, u, 1, 1) * factor).astype(BF16)
    rebuilt = (two[...].astype(F32) - c[...] * mask).astype(BF16)
    two_out[...] = rebuilt
    total_out[...] = (cot_one[...].astype(F32) + d[...]).astype(BF16)
    left_out[...] = dot(pick_left[...], rebuilt, 1, 1).astype(BF16)
    right_out[...] = dot(pick_right[...], rebuilt, 1, 1).astype(BF16)


def halo_kernel(nx, ny, tile, left, right, north, south, edges, send_sem, recv_sem):
    i = lax.axis_index("gx")
    j = lax.axis_index("gy")
    east, west = lax.rem(i + 1, nx), lax.rem(i + nx - 1, nx)
    mirror = nx - 1 - i
    beyond, before = lax.rem(mirror + 1, nx), lax.rem(mirror + nx - 1, nx)
    top = j == ny - 1
    inner = j < ny - 1
    raised = j > 0

    sends = [
        (None, right, edges.at[WEST], 0, east, j),
        (None, left, edges.at[EAST], 1, west, j),
        (raised, tile, north, 2, i, j - 1),
        (raised, right, edges.at[NORTH_WEST], 3, east, j - 1),
        (raised, left, edges.at[NORTH_EAST], 4, west, j - 1),
        (inner, tile, south, 5, i, j + 1),
        (inner, right, edges.at[SOUTH_WEST], 6, east, j + 1),
        (inner, left, edges.at[SOUTH_EAST], 7, west, j + 1),
        (top, tile, north, 2, mirror, j),
        (top & (beyond != i), left, edges.at[NORTH_WEST], 3, beyond, j),
        (top & (before != i), right, edges.at[NORTH_EAST], 4, before, j),
    ]

    def guarded(active, run):
        if active is None:
            run()
        else:
            pl.when(active)(run)

    def copy_of(k):
        active, source, target, number, x, y = sends[k]
        return pltpu.make_async_remote_copy(
            src_ref=source,
            dst_ref=target,
            send_sem=send_sem.at[k],
            recv_sem=recv_sem.at[number],
            device_id=(x, y),
            device_id_type=MESH,
        )

    barrier = pltpu.get_barrier_semaphore()
    for active, _, _, _, x, y in sends:

        def tell(x=x, y=y):
            pl.semaphore_signal(barrier, inc=1, device_id=(x, y), device_id_type=MESH)

        guarded(active, tell)
    one_if = lambda flag: flag.astype(jnp.int32)
    peers = 5 + 3 * one_if(raised) - one_if(top & (beyond == i)) - one_if(top & (before == i))
    pl.semaphore_wait(barrier, peers)
    order = [2, 5, 8, 0, 1, 3, 4, 6, 7, 9, 10]
    for k in order:
        guarded(sends[k][0], lambda k=k: copy_of(k).start())

    @pl.when(top & (beyond == i))
    def _():
        edges[NORTH_WEST] = left[...]

    @pl.when(top & (before == i))
    def _():
        edges[NORTH_EAST] = right[...]

    for k in order:
        guarded(sends[k][0], lambda k=k: copy_of(k).wait_send())
    arrivals = [
        (None, 0), (None, 1), (raised, 5), (raised, 6), (raised, 7),
        (inner, 2), (inner, 3), (inner, 4), (top, 8),
        (top & (beyond != i), 9), (top & (before != i), 10),
    ]
    for active, k in arrivals:
        guarded(active, lambda k=k: copy_of(k).wait_recv())


def load_field(own, north, south, edges, turn, place_mid, place_north, place_south, flags, mid, rim):
    channels, cells = own.shape
    has_south = flags[0] > 0
    mid[0, :channels, :] = jnp.where(has_south, south[...].astype(F32), 0.0)
    mid[1, :channels, :] = own[...].astype(F32)
    mid[2, :channels, :] = dot(north[...], turn[...], 1, 0)
    pairs = (
        (SOUTH_WEST, SOUTH_EAST, place_south),
        (WEST, EAST, place_mid),
        (NORTH_WEST, NORTH_EAST, place_north),
    )
    for group, (west, east, place) in enumerate(pairs):
        side = dot(edges[west], place[0], 0, 0) + dot(edges[east], place[1], 0, 0)
        if group == 0:
            side = jnp.where(has_south, side, 0.0)
        rim[group, :channels, :] = side


def shifted_rows(mid, rim, rows, columns, offset):
    lane = lax.broadcasted_iota(jnp.int32, (8, columns), 1)
    out = []
    for p in range(9):
        cols = pl.ds((p % 3) * columns, columns)
        center = mid[p // 3, rows, cols]
        if offset == 0:
            out.append(center)
            continue
        side = rim[p // 3, rows, cols]
        outside = lane < offset if offset > 0 else lane >= columns + offset
        out.append(pltpu.roll(jnp.where(outside, side, center), (-offset) % columns, 1))
    return out


def convolve(mid, rim, weights, north_weights, out, columns):
    blocks = mid.shape[1] // 8

    def step(i, carry):
        rows = pl.ds(pl.multiple_of(i * 8, 8), 8)
        w = weights[rows, :]
        wn = north_weights[rows, :]
        acc = [jnp.zeros((8, columns), F32) for _ in range(3)]
        for col in range(TAPS):
            field = shifted_rows(mid, rim, rows, columns, col - REACH)
            for row in range(TAPS):
                t = row * TAPS + col
                k = jnp.broadcast_to(w[:, t : t + 1], (8, columns))
                kn = jnp.broadcast_to(wn[:, t : t + 1], (8, columns)) if row > 3 else None
                for r in range(3):
                    acc[r] = acc[r] + (kn if r + row >= 6 else k) * field[r + row]
        for r in range(3):
            out[rows, r * columns : (r + 1) * columns] = acc[r]
        return carry

    lax.fori_loop(0, blocks, step, 0)


def correlate(mid, rim, back, out, columns):
    blocks = mid.shape[1] // 8

    def step(i, carry):
        rows = pl.ds(pl.multiple_of(i * 8, 8), 8)
        lane = lax.broadcasted_iota(jnp.int32, (8, columns), 1)
        g = [back[rows, r * columns : (r + 1) * columns] for r in range(3)]
        total = jnp.zeros((8, columns), F32)
        for col in range(TAPS):
            field = shifted_rows(mid, rim, rows, columns, col - REACH)
            for row in range(TAPS):
                part = g[0] * field[row] + g[1] * field[row + 1] + g[2] * field[row + 2]
                summed = jnp.sum(part, axis=1, keepdims=True)
                total = jnp.where(lane == row * TAPS + col, summed, total)
        out[rows, :] = total
        return carry

    lax.fori_loop(0, blocks, step, 0)


def mixer_kernel(
    factor, columns, flags, own, north, south, edges, turn, place_mid, place_north, place_south,
    one, total, mask_in, weights, ew, rw, pick_left, pick_right,
    one_out, back_out, left_out, right_out, gk, ge, gr,
    mid, rim, spread, pre, back, act, bp, gk_wide,
):
    channels, cells = own.shape
    load_field(own, north, south, edges, turn, place_mid, place_north, place_south, flags, mid, rim)
    mask = mask_in[0:1, :]
    upstream = (total[...].astype(F32) * mask).astype(BF16)
    back[...] = dot(rw[...], upstream, 1, 0)
    convolve(mid, rim, weights, weights, spread, columns)
    field = spread[:channels, :]
    center = field - jnp.mean(field, axis=0, keepdims=True)
    rescale = lax.rsqrt(jnp.mean(center * center, axis=0, keepdims=True) + EPSILON)
    normal = center * rescale
    spread[:channels, :] = normal
    half = normal.astype(BF16)
    pre[...] = dot(ew[...], half, 0, 0)
    activate(pre, back, act, bp)
    back_normal = dot(ew[...], bp[...], 1, 0)
    normal = spread[:channels, :]
    mean_back = jnp.mean(back_normal, axis=0, keepdims=True)
    mean_cross = jnp.mean(back_normal * normal, axis=0, keepdims=True)
    back_spread = (rescale * (back_normal - mean_back - normal * mean_cross)).astype(BF16)
    back_out[...] = back_spread
    left_out[...] = dot(pick_left[...], back_spread, 1, 1).astype(BF16)
    right_out[...] = dot(pick_right[...], back_spread, 1, 1).astype(BF16)
    ge[...] = (dot(normal.astype(BF16), bp[...], 1, 1) * factor).astype(BF16)
    gr[...] = (dot(act[...], upstream, 1, 1) * factor).astype(BF16)
    update = dot(rw[...], act[...], 0, 0)
    one_out[...] = (one[...].astype(F32) - update * mask).astype(BF16)
    spread[:channels, :] = back_spread.astype(F32)
    correlate(mid, rim, spread, gk_wide, columns)
    gk[...] = (gk_wide[:channels, :] * factor).astype(BF16)


def back_kernel(
    columns, flags, own, north, south, edges, turn, place_mid, place_north, place_south,
    cot_two, weights, north_weights, out, mid, rim, through,
):
    channels, cells = own.shape
    load_field(own, north, south, edges, turn, place_mid, place_north, place_south, flags, mid, rim)
    convolve(mid, rim, weights, north_weights, through, columns)
    out[...] = (cot_two[...].astype(F32) + through[:channels, :]).astype(BF16)


def placements(rows, columns):
    cells = rows * columns
    pick_left = np.zeros((EDGE_ROWS, cells), np.float32)
    pick_right = np.zeros((EDGE_ROWS, cells), np.float32)
    place = np.zeros((2, EDGE_ROWS, cells), np.float32)
    folded = np.zeros((2, EDGE_ROWS, cells), np.float32)
    for r in range(rows):
        for c in range(REACH):
            e = r * REACH + c
            pick_left[e, r * columns + c] = 1
            pick_right[e, r * columns + columns - REACH + c] = 1
            place[0, e, r * columns + columns - REACH + c] = 1
            place[1, e, r * columns + c] = 1
            turned = rows - 1 - r
            folded[0, e, turned * columns + columns - 1 - c] = 1
            folded[1, e, turned * columns + REACH - 1 - c] = 1
    return pick_left, pick_right, place, folded


def body(
    output_one, output_two, cotan_one, cotan_two, wet_list, depth_kernel,
    expand_weight, reduce_weight, level_expand, level_reduce,
):
    channels, rows, columns = output_one.shape
    cells = rows * columns
    groups, levels, width = level_expand.shape
    hidden = expand_weight.shape[1]
    nx, ny = lax.axis_size("gx"), lax.axis_size("gy")
    factor = 1.0 / math.sqrt(cells * nx * ny)
    wide = -(-channels // 8) * 8
    slot = -(-width // 16) * 16
    i, j = lax.axis_index("gx"), lax.axis_index("gy")
    top = j == ny - 1
    flags = jnp.stack([(j > 0).astype(jnp.int32), top.astype(jnp.int32)])

    pick_left, pick_right, place, folded = [jnp.asarray(m, BF16) for m in placements(rows, columns)]
    place_north = jnp.where(top, folded, place)
    row_id = lax.broadcasted_iota(jnp.int32, (cells, cells), 0)
    col_id = lax.broadcasted_iota(jnp.int32, (cells, cells), 1)
    turn = jnp.where(jnp.where(top, cells - 1 - row_id, row_id) == col_id, 1.0, 0.0).astype(BF16)

    flat = lambda x: x.reshape(channels, cells)
    tile = jax.ShapeDtypeStruct((channels, cells), BF16)
    edge = jax.ShapeDtypeStruct((EDGE_ROWS, channels), BF16)
    vmem = pl.BlockSpec(memory_space=pltpu.VMEM)
    smem = pl.BlockSpec(memory_space=pltpu.SMEM)
    params = pltpu.CompilerParams(vmem_limit_bytes=56 * 1024 * 1024)

    one, two, cot_one, cot_two = flat(output_one), flat(output_two), flat(cotan_one), flat(cotan_two)
    two_in, total, left, right, mask, gle, glr = pl.pallas_call(
        functools.partial(level_kernel, factor, slot),
        out_shape=(
            tile, tile, edge, edge,
            jax.ShapeDtypeStruct((8, cells), F32),
            jax.ShapeDtypeStruct(level_expand.shape, BF16),
            jax.ShapeDtypeStruct(level_reduce.shape, BF16),
        ),
        in_specs=[vmem] * 9,
        out_specs=(vmem,) * 7,
        scratch_shapes=[pltpu.VMEM((channels, cells), F32)] * 4
        + [pltpu.VMEM((groups * slot, cells), F32)] * 2
        + [pltpu.VMEM((groups * slot, cells), BF16)] * 2,
        compiler_params=params,
        name="level",
    )(one, two, cot_one, cot_two, wet_list.reshape(-1, 1), level_expand, level_reduce, pick_left, pick_right)
    gle, glr = lax.psum((gle, glr), ("gx", "gy"))

    halo = pl.pallas_call(
        functools.partial(halo_kernel, nx, ny),
        out_shape=(tile, tile, jax.ShapeDtypeStruct((6, EDGE_ROWS, channels), BF16)),
        in_specs=[vmem] * 3,
        out_specs=(vmem,) * 3,
        scratch_shapes=[pltpu.SemaphoreType.DMA((11,)), pltpu.SemaphoreType.DMA((8,))],
        compiler_params=pltpu.CompilerParams(collective_id=0, has_side_effects=True),
        name="halo",
    )
    north, south, edges = halo(two_in, left, right)

    taps = depth_kernel.astype(F32).reshape(channels, TAPS * TAPS)
    pad = lambda w: jnp.pad(w, ((0, wide - channels), (0, 128 - TAPS * TAPS)))
    field_scratch = [pltpu.VMEM((3, wide, cells), F32)] * 2 + [pltpu.VMEM((wide, cells), F32)]
    one_in, back, back_left, back_right, gk, ge, gr = pl.pallas_call(
        functools.partial(mixer_kernel, factor, columns),
        out_shape=(
            tile, tile, edge, edge,
            jax.ShapeDtypeStruct((channels, 128), BF16),
            jax.ShapeDtypeStruct(expand_weight.shape, BF16),
            jax.ShapeDtypeStruct(reduce_weight.shape, BF16),
        ),
        in_specs=[smem] + [vmem] * 16,
        out_specs=(vmem,) * 7,
        scratch_shapes=field_scratch
        + [pltpu.VMEM((hidden, cells), F32)] * 2
        + [pltpu.VMEM((hidden, cells), BF16)] * 2
        + [pltpu.VMEM((wide, 128), F32)],
        compiler_params=params,
        name="mixer",
    )(
        flags, two_in, north, south, edges, turn, place, place_north, place, one, total, mask,
        pad(taps), expand_weight, reduce_weight, pick_left, pick_right,
    )
    gk, ge, gr = lax.psum((gk, ge, gr), ("gx", "gy"))

    north, south, edges = halo(back, back_left, back_right)
    flipped = taps[:, ::-1]
    grad_two = pl.pallas_call(
        functools.partial(back_kernel, columns),
        out_shape=tile,
        in_specs=[smem] + [vmem] * 11,
        out_specs=vmem,
        scratch_shapes=field_scratch,
        compiler_params=params,
        name="back",
    )(
        flags, back, north, south, edges, turn, place, place_north, place, cot_two,
        pad(flipped), pad(jnp.where(top, taps, flipped)),
    )
    grid = lambda x: x.reshape(channels, rows, columns)
    gk = gk[:, : TAPS * TAPS].astype(F32).reshape(channels, TAPS, TAPS)
    return (
        grid(one_in), grid(two_in), grid(total), grid(grad_two),
        gk, ge.astype(F32), gr.astype(F32), gle.astype(F32), glr.astype(F32),
    )


def solution(mesh):
    field = P(None, "gy", "gx")
    return jax.shard_map(
        body,
        mesh=mesh,
        in_specs=(field,) * 4 + (P("gy", "gx", None, None),) + (P(),) * 5,
        out_specs=(field,) * 4 + (P(),) * 5,
        check_vma=False,
    )
```

time: 480 us -> 226 us (0.47); the launches traced: 473 us -> 225 us
  other arithmetic: 232 us -> 5.42 us
  Pallas kernels: 0 us -> 73.5 us
  blocking collectives: 41.8 us -> 0 us
  local copies, waits for them, and re-layouts: 44 us -> 20.6 us
  starting transfers between devices: 20.4 us -> 0.04 us
  matrix products: 19.1 us -> 0 us
  waiting for transfers between devices: 98.9 us -> 111 us
    reduce_sum x6 -> x0, other arithmetic: 139 us -> none  [the longest x3 102 us: body(): jnp.sum(back_field * wide_field[:, row_tap:row_tap + tile_rows, col_tap:c...]
    psum x1, waiting for transfers between devices: 28.6 us -> 111 us  [body(): gk, ge, gr = lax.psum((gk, ge, gr), ('gx', 'gy'))]
    pallas_call x0 -> x5, Pallas kernels: none -> 73.5 us  [the longest x1 32.4 us: body(): pl.pallas_call(functools.partial(mixer_kernel, factor, columns), out_shap...]
    ppermute x14 -> x0, waiting for transfers between devices: 70.3 us -> none  [the longest x6 43.3 us: swapped(): lax.ppermute(shard, axis, [(i, i ^ 1 << stride) for i in range(lax.axis_s...]
    convert_element_type x11 -> x2, other arithmetic: 49.8 us -> 3.2 us  [the longest x1 2.37 us: body(): ge.astype(F32)]
    psum x1 -> x0, blocking collectives: 41.8 us -> none  [body(): lax.psum((grad_kernel, grad_expand, grad_reduce, grad_level_in, grad_leve...]
    add x3 -> x0, other arithmetic: 28 us -> none  [body(): row_total + kernel_wide[:, row_tap, col_tap][:, None] * turned[:, source_...]
    ppermute x14 -> x0, starting transfers between devices: 20.3 us -> none  [the longest x6 7.85 us: swapped(): lax.ppermute(shard, axis, [(i, i ^ 1 << stride) for i in range(lax.axis_s...]
  transfers between devices with their start and end apart: 15 -> 1, of which waited for: 13 -> 1; matrix products, arithmetic and copies ran while one was open for 19% -> 3% of each run, Pallas kernels for 0% -> 11%
where the time goes in v1:
time: 226 us; the launch traced here: 225 us
  waiting for transfers between devices  111 us (49%)
  Pallas kernels  73.5 us (33%)
  local copies, waits for them, and re-layouts  20.6 us (9%)
  between operations  14.3 us (6%)
  other arithmetic  5.42 us (2%)
    psum x1, waiting for transfers between devices, body(): gk, ge, gr = lax.psum((gk, ge, gr), ('gx', 'gy'))  111 us
    pallas_call x1, Pallas kernels, body(): pl.pallas_call(functools.partial(mixer_kernel, factor, columns), out_shap...  32.4 us
    unnamed x54, local copies, waits for them, and re-layouts  15.3 us
    pallas_call x1, Pallas kernels, body(): pl.pallas_call(functools.partial(back_kernel, columns), out_shape=tile, i...  12.8 us
    pallas_call x1, Pallas kernels, body(): north, south, edges = halo(back, back_left, back_right)  11.5 us
    pallas_call x1, Pallas kernels, body(): north, south, edges = halo(two_in, left, right)  10.7 us
    pallas_call x1, Pallas kernels, body(): pl.pallas_call(functools.partial(level_kernel, factor, slot), out_shape=(...  6.14 us
  transfers between devices with their start and end apart: 1, of which 1 were waited for; matrix products, arithmetic and copies ran while one was open for 3% of the time, Pallas kernels for 11%

profile of v1, /device:TPU:0, one launch (start us, length us, event | category | flops | bytes accessed | tf_op | source)
XLA Modules:
  0.0 225.3 jit_solution(6130048714225599331)
XLA Ops:
  7.2 0.0 all-reduce.6.cloned.1.call-start
  7.2 1.1 copy.58
  8.4 0.1 pad.15
  8.5 0.7 copy.77
  9.2 0.1 copy.59
  9.4 0.1 pad.16
  9.5 0.7 copy.78
  10.2 0.1 copy.60
  10.4 0.1 pad.17
  10.5 0.7 copy.79
  11.2 0.1 copy.61
  11.4 0.1 pad.18
  11.5 0.7 copy.80
  12.2 0.8 reshape.74.listing
  13.0 0.7 copy.63.le
  13.8 1.0 copy.64.lr
  14.8 0.8 select_convert_fusion.turn
  15.6 0.1 copy.65
  15.7 1.3 copy.66.rw
  17.0 0.6 add_convert_fusion.flags
  17.6 0.6 broadcast_select_fusion.1.place_north
  18.2 0.7 pad.10.weights
  18.9 6.1 %level.1 = (bf16[300,384]{1,0:T(8,128)(2,1)}, bf16[300,384]{1,0:T(8,128)(2,1)}, bf16[16,300]{1,0:T(8,128)(2,1)}, bf16[16,300]{1,0:T(8,128)(2,1)}, f32[8,384]{1,0...) custom-call(bf16[300,384]{1,0:T(8,128)(2,1)} %bitcast.20, bf16[300,384]{1,0:T(8,128)(2,1)} %bitcast.28, ...), custom_call_target="tpu_custom_call" | custom-call | tf_op jit(solution)/shard_map/level/pallas_call | solution.py:321
  25.0 10.7 %halo.2 = (bf16[300,384]{1,0:T(8,128)(2,1)}, bf16[300,384]{1,0:T(8,128)(2,1)}, bf16[6,16,300]{2,1,0:T(8,128)(2,1)}) custom-call(bf16[300,384]{1,0:T(8,128)(2,1)} %get-tuple-element.29.tile.own, bf16[16,300]{1,0:T(8,128)(2,1)} %get-tuple-element.30.left, bf16[16,300]{1,0:T(8,128)(2,1)} %get-tuple-element.31.right), custom_call_target="tpu_custom_call" | custom-call | tf_op jit(solution)/shard_map/halo/pallas_call | solution.py:348
  35.7 32.4 %mixer.1 = (bf16[300,384]{1,0:T(8,128)(2,1)}, bf16[300,384]{1,0:T(8,128)(2,1)}, bf16[16,300]{1,0:T(8,128)(2,1)}, bf16[16,300]{1,0:T(8,128)(2,1)}, bf16[300,128]{...) custom-call(s32[2]{0:T(128)} %add_convert_fusion.flags, ...), custom_call_target="tpu_custom_call" | custom-call | tf_op jit(solution)/shard_map/mixer/pallas_call | solution.py:353
  68.2 0.9 copy-done
  69.0 0.1 reshape.65
  69.1 0.0 copy-done.1
  69.2 0.1 reshape.66
  69.2 0.4 rev.3
  69.7 0.1 reshape.64
  69.7 0.7 copy.70
  70.5 0.7 copy.71
  71.2 0.7 copy.72
  71.9 0.7 pad.11.weights
  72.6 0.7 pad.12.north_weights
  73.3 11.5 %halo.3 = (bf16[300,384]{1,0:T(8,128)(2,1)}, bf16[300,384]{1,0:T(8,128)(2,1)}, bf16[6,16,300]{2,1,0:T(8,128)(2,1)}) custom-call(bf16[300,384]{1,0:T(8,128)(2,1)} %get-tuple-element.38.tile.own, bf16[16,300]{1,0:T(8,128)(2,1)} %get-tuple-element.39.left, bf16[16,300]{1,0:T(8,128)(2,1)} %get-tuple-element.40.right), custom_call_target="tpu_custom_call" | custom-call | tf_op jit(solution)/shard_map/halo/pallas_call | solution.py:375
  84.8 12.8 %back.1 = bf16[300,384]{1,0:T(8,128)(2,1)} custom-call(s32[2]{0:T(128)} %add_convert_fusion.flags, bf16[300,384]{1,0:T(8,128)(2,1)} %get-tuple-element.38.tile.own, bf16[300,384]{1,0:T(8,128)(2,1)} %get-tuple-element.41.north, bf16[300,384]{1,0:T(8,128)(2,1)} %get-tuple-element.42.south, bf16[6,16,300]{2,1,0:T(8,128)(2,1)} %get-tuple-element.43.edges, ...), custom_call_target="tpu_custom_call" | custom-call | tf_op jit(solution)/shard_map/back/pallas_call | solution.py:377
  97.6 1.0 reshape.67
  98.6 0.7 copy.73
  99.4 111.4 %all-reduce.6.cloned.1.call-done = (bf16[1200,300]{1,0:T(8,128)(2,1)}, bf16[4,75,300]{2,1,0:T(8,128)(2,1)}, bf16[4,300,75]{2,1,0:T(8,128)(2,1)}, bf16[300,128]{1,0:T(8,128)(2,1)}, bf16[300,1200]{1,0:T(8,128)(2,1)}) async-done(((bf16[1200,300]{1,0:T(8,128)(2,1)}, bf16[4,75,300]{2,1,0:T(8,128)(2,1)}, bf16[4,300,75]{2,1,0:T(8,128)(2,1)}, bf16[300,128]{1,0:T(8,128)(2,1)}, bf16[300,1200]{1,0:T(8,128)(2,1)}), ...) | async-done | bytes 1876816 | tf_op jit(solution)/shard_map/psum | solution.py:373
  210.8 1.0 slice_convert_fusion
  211.8 0.1 copy.69
  211.9 0.7 reshape.73
  212.5 2.4 %convert_element_type.24 = f32[300,1200]{1,0:T(8,128)} convert(bf16[300,1200]{1,0:T(8,128)(2,1)} %get-tuple-element.80) | non-fusion elementwise | flops 360000 | bytes 2160000 | tf_op jit(solution)/shard_map/convert_element_type | solution.py:393
  214.9 1.7 copy.74
  216.6 0.9 copy.75
  217.5 1.0 copy.76
  (34 shorter events, 0.1 us)
Async XLA Ops:
  7.2 2.0 copy-start.7
  7.2 203.6 %all-reduce.6.cloned.1.call-start = ((), (), s32[]{:S(2)}) async-start(), calls=%async_computation | async-start | bytes 4669440 | tf_op jit(solution)/shard_map/psum | solution.py:373
  8.3 1.9 copy-start.8
  9.3 1.9 copy-start.9
  10.3 1.9 copy-start.15
  10.4 2.7 %copy-start.11 = (bf16[4,75,300]{2,0,1:T(4,128)(2,1)S(1)}, bf16[4,75,300]{2,0,1:T(4,128)(2,1)}, u32[]{:S(2)}) copy-start(bf16[4,75,300]{2,0,1:T(4,128)(2,1)} %param.22) | copy-start | bytes 540004
  10.5 3.3 %copy-start.12 = (bf16[4,300,75]{1,0,2:T(4,128)(2,1)S(1)}, bf16[4,300,75]{1,0,2:T(4,128)(2,1)}, u32[]{:S(2)}) copy-start(bf16[4,300,75]{1,0,2:T(4,128)(2,1)} %param.23) | copy-start | bytes 540004
  11.2 4.4 %copy-start.13 = (bf16[300,7,7]{0,2,1:T(8,128)(2,1)S(1)}, bf16[300,7,7]{0,2,1:T(8,128)(2,1)}, u32[]{:S(2)}) copy-start(bf16[300,7,7]{0,2,1:T(8,128)(2,1)} %param.19) | copy-start | bytes 88204
  11.4 4.4 %copy-start.3 = (bf16[1200,300]{0,1:T(8,128)(2,1)S(1)}, bf16[1200,300]{0,1:T(8,128)(2,1)}, u32[]{:S(2)}) copy-start(bf16[1200,300]{0,1:T(8,128)(2,1)} %param.21) | copy-start | bytes 2160004
  13.8 3.9 %copy-start.4 = (bf16[2,16,384]{2,1,0:T(8,128)(2,1)S(1)}, bf16[2,16,384]{2,1,0:T(8,128)(2,1)}, u32[]{:S(2)}) copy-start(bf16[2,16,384]{2,1,0:T(8,128)(2,1)} %constant.25.clone.place_mid.place_south) | copy-start | bytes 73732
  13.8 3.9 %copy-start.14 = (bf16[2,16,384]{2,1,0:T(8,128)(2,1)S(1)}, bf16[2,16,384]{2,1,0:T(8,128)(2,1)}, u32[]{:S(2)}) copy-start(bf16[2,16,384]{2,1,0:T(8,128)(2,1)} %constant.26.clone) | copy-start | bytes 73732
  68.1 0.9 copy-start
  68.1 1.0 copy-start.1
  68.1 1.5 copy-start.10
  210.8 4.1 %copy-start.2 = (bf16[1200,300]{1,0:T(8,128)(2,1)S(1)}, bf16[1200,300]{1,0:T(8,128)(2,1)}, u32[]{:S(2)}) copy-start(bf16[1200,300]{1,0:T(8,128)(2,1)} %get-tuple-element.76) | copy-start | bytes 2160004
  214.9 1.7 copy-start.6
  214.9 2.6 %copy-start.5 = (bf16[4,300,75]{2,1,0:T(8,128)(2,1)S(1)}, bf16[4,300,75]{2,1,0:T(8,128)(2,1)}, u32[]{:S(2)}) copy-start(bf16[4,300,75]{2,1,0:T(8,128)(2,1)} %get-tuple-element.78) | copy-start | bytes 540004
Sparse Core Ops, SparseCore 0:
  68.3 142.4 all-reduce.5

commit v2 on v1

--- a/solution.py
+++ b/solution.py
@@ -63,8 +63,8 @@
         bp_v = bp[v * slot : v * slot + width, :]
         c[v * levels : (v + 1) * levels, :] = dot(lr[v], act_v, 0, 0)
         d[v * levels : (v + 1) * levels, :] = dot(le[v], bp_v, 1, 0)
-        gle[v] = (dot(g, bp_v, 1, 1) * factor).astype(BF16)
-        glr[v] = (dot(act_v, u, 1, 1) * factor).astype(BF16)
+        gle[v] = dot(g, bp_v, 1, 1) * factor
+        glr[v] = dot(act_v, u, 1, 1) * factor
     rebuilt = (two[...].astype(F32) - c[...] * mask).astype(BF16)
     two_out[...] = rebuilt
     total_out[...] = (cot_one[...].astype(F32) + d[...]).astype(BF16)
@@ -144,6 +144,84 @@
     ]
     for active, k in arrivals:
         guarded(active, lambda k=k: copy_of(k).wait_recv())
+
+
+def sum_kernel(dims, pack, out, work, held, send_sem, recv_sem):
+    place = (lax.axis_index("gx"), lax.axis_index("gy"))
+    steps = len(dims)
+    lanes = pack.shape[2] // 3
+    bits, peers = [], []
+    for axis, k in dims:
+        bit = lax.rem(place[axis] // (1 << k), 2)
+        bits.append(bit)
+        other = place[axis] + (1 - 2 * bit) * (1 << k)
+        peers.append((other, place[1]) if axis == 0 else (place[0], other))
+    barrier = pltpu.get_barrier_semaphore()
+    for peer in peers:
+        pl.semaphore_signal(barrier, inc=1, device_id=peer, device_id_type=MESH)
+    pl.semaphore_wait(barrier, steps)
+    rest = steps - 1
+    orders = [[0] + [1 + (k + s) % rest for k in range(rest)] for s in range(3)]
+    base = [0, 0, 0]
+    trail = []
+    size = pack.shape[0]
+    offset = 0
+    for step in range(steps):
+        size //= 2
+        copies = []
+        source = pack if step == 0 else work
+        target = out if step == steps - 1 else work
+        ranges = []
+        for s in range(3):
+            d = orders[s][step]
+            cols = pl.ds(s * lanes, lanes)
+            keep = base[s] + bits[d] * size
+            give = base[s] + (1 - bits[d]) * size
+            ranges.append((keep, give))
+            copy = pltpu.make_async_remote_copy(
+                src_ref=source.at[pl.ds(give, size), :, cols],
+                dst_ref=held.at[pl.ds(offset, size), :, cols],
+                send_sem=send_sem.at[s, step],
+                recv_sem=recv_sem.at[s, step],
+                device_id=peers[d],
+                device_id_type=MESH,
+            )
+            copy.start()
+            copies.append(copy)
+        for s in range(3):
+            copies[s].wait_recv()
+            cols = pl.ds(s * lanes, lanes)
+            keep = ranges[s][0]
+
+            def add(c, carry, cols=cols, keep=keep, source=source, target=target, offset=offset):
+                mine = source[keep + c, :, cols].astype(F32)
+                target[keep + c, :, cols] = (mine + held[offset + c, :, cols].astype(F32)).astype(BF16)
+                return carry
+
+            lax.fori_loop(0, size, add, 0)
+            base[s] = keep
+        for copy in copies:
+            copy.wait_send()
+        trail.append((size, ranges))
+        offset += size
+    for step in reversed(range(steps)):
+        size, ranges = trail[step]
+        copies = []
+        for s in range(3):
+            cols = pl.ds(s * lanes, lanes)
+            part = out.at[pl.ds(ranges[s][0], size), :, cols]
+            copy = pltpu.make_async_remote_copy(
+                src_ref=part,
+                dst_ref=part,
+                send_sem=send_sem.at[s, steps + step],
+                recv_sem=recv_sem.at[s, steps + step],
+                device_id=peers[orders[s][step]],
+                device_id_type=MESH,
+            )
+            copy.start()
+            copies.append(copy)
+        for copy in copies:
+            copy.wait()
 
 
 def load_field(own, north, south, edges, turn, place_mid, place_north, place_south, flags, mid, rim):
@@ -225,7 +303,7 @@
 def mixer_kernel(
     factor, columns, flags, own, north, south, edges, turn, place_mid, place_north, place_south,
     one, total, mask_in, weights, ew, rw, pick_left, pick_right,
-    one_out, back_out, left_out, right_out, gk, ge, gr,
+    one_out, back_out, left_out, right_out, pack,
     mid, rim, spread, pre, back, act, bp, gk_wide,
 ):
     channels, cells = own.shape
@@ -250,13 +328,18 @@
     back_out[...] = back_spread
     left_out[...] = dot(pick_left[...], back_spread, 1, 1).astype(BF16)
     right_out[...] = dot(pick_right[...], back_spread, 1, 1).astype(BF16)
-    ge[...] = (dot(normal.astype(BF16), bp[...], 1, 1) * factor).astype(BF16)
-    gr[...] = (dot(act[...], upstream, 1, 1) * factor).astype(BF16)
+    units = bp.shape[0]
+    half_lanes = pack.shape[1] // 2
+    pack[:units, :channels] = (dot(bp[...], normal.astype(BF16), 1, 1) * factor).astype(BF16)
+    pack[:units, half_lanes : half_lanes + channels] = (dot(act[...], upstream, 1, 1) * factor).astype(BF16)
     update = dot(rw[...], act[...], 0, 0)
     one_out[...] = (one[...].astype(F32) - update * mask).astype(BF16)
     spread[:channels, :] = back_spread.astype(F32)
     correlate(mid, rim, spread, gk_wide, columns)
-    gk[...] = (gk_wide[:channels, :] * factor).astype(BF16)
+    spare = pack.shape[0] - units
+    pick = lax.broadcasted_iota(jnp.int32, (spare, columns), 0) == lax.broadcasted_iota(jnp.int32, (spare, columns), 1)
+    taps = (gk_wide[:channels, :] * factor).astype(BF16)
+    pack[units:, :channels] = dot(jnp.where(pick, 1.0, 0.0).astype(BF16), taps, 1, 1).astype(BF16)
 
 
 def back_kernel(
@@ -323,8 +406,8 @@
         out_shape=(
             tile, tile, edge, edge,
             jax.ShapeDtypeStruct((8, cells), F32),
-            jax.ShapeDtypeStruct(level_expand.shape, BF16),
-            jax.ShapeDtypeStruct(level_reduce.shape, BF16),
+            jax.ShapeDtypeStruct(level_expand.shape, F32),
+            jax.ShapeDtypeStruct(level_reduce.shape, F32),
         ),
         in_specs=[vmem] * 9,
         out_specs=(vmem,) * 7,
@@ -350,16 +433,19 @@
     taps = depth_kernel.astype(F32).reshape(channels, TAPS * TAPS)
     pad = lambda w: jnp.pad(w, ((0, wide - channels), (0, 128 - TAPS * TAPS)))
     field_scratch = [pltpu.VMEM((3, wide, cells), F32)] * 2 + [pltpu.VMEM((wide, cells), F32)]
-    one_in, back, back_left, back_right, gk, ge, gr = pl.pallas_call(
+    chunks = nx * ny
+    spare_rows = TAPS * TAPS
+    chunk_rows = -(-(hidden + spare_rows) // (8 * chunks)) * 8
+    half_lanes = -(-channels // 384) * 384
+    lanes = 2 * half_lanes
+    one_in, back, back_left, back_right, pack = pl.pallas_call(
         functools.partial(mixer_kernel, factor, columns),
         out_shape=(
             tile, tile, edge, edge,
-            jax.ShapeDtypeStruct((channels, 128), BF16),
-            jax.ShapeDtypeStruct(expand_weight.shape, BF16),
-            jax.ShapeDtypeStruct(reduce_weight.shape, BF16),
+            jax.ShapeDtypeStruct((chunks * chunk_rows, lanes), BF16),
         ),
         in_specs=[smem] + [vmem] * 16,
-        out_specs=(vmem,) * 7,
+        out_specs=(vmem,) * 5,
         scratch_shapes=field_scratch
         + [pltpu.VMEM((hidden, cells), F32)] * 2
         + [pltpu.VMEM((hidden, cells), BF16)] * 2
@@ -370,7 +456,27 @@
         flags, two_in, north, south, edges, turn, place, place_north, place, one, total, mask,
         pad(taps), expand_weight, reduce_weight, pick_left, pick_right,
     )
-    gk, ge, gr = lax.psum((gk, ge, gr), ("gx", "gy"))
+    dims = [(1, k) for k in range(ny.bit_length() - 1)] + [(0, k) for k in range(nx.bit_length() - 1)]
+    pack = pack.reshape(chunks, chunk_rows, lanes)
+    summed = pl.pallas_call(
+        functools.partial(sum_kernel, dims),
+        out_shape=jax.ShapeDtypeStruct(pack.shape, BF16),
+        in_specs=[vmem],
+        out_specs=vmem,
+        scratch_shapes=[
+            pltpu.VMEM(pack.shape, BF16),
+            pltpu.VMEM(pack.shape, BF16),
+            pltpu.SemaphoreType.DMA((3, 2 * len(dims))),
+            pltpu.SemaphoreType.DMA((3, 2 * len(dims))),
+        ],
+        compiler_params=pltpu.CompilerParams(
+            collective_id=1, has_side_effects=True, vmem_limit_bytes=56 * 1024 * 1024
+        ),
+        name="sum",
+    )(pack).reshape(chunks * chunk_rows, lanes)
+    ge = summed[:hidden, :channels].T
+    gr = summed[:hidden, half_lanes : half_lanes + channels]
+    gk = summed[hidden : hidden + spare_rows, :channels].T
 
     north, south, edges = halo(back, back_left, back_right)
     flipped = taps[:, ::-1]
@@ -390,7 +496,7 @@
     gk = gk[:, : TAPS * TAPS].astype(F32).reshape(channels, TAPS, TAPS)
     return (
         grid(one_in), grid(two_in), grid(total), grid(grad_two),
-        gk, ge.astype(F32), gr.astype(F32), gle.astype(F32), glr.astype(F32),
+        gk, ge.astype(F32), gr.astype(F32), gle, glr,
     )
 
 

time: 226 us -> 170 us (0.75)
  waiting for transfers between devices: 111 us -> 1.93 us
  Pallas kernels: 73.5 us -> 123 us
  local copies, waits for them, and re-layouts: 20.6 us -> 24.4 us
    psum x1, waiting for transfers between devices: 111 us -> 1.91 us  [body(): gle, glr = lax.psum((gle, glr), ('gx', 'gy'))]
    pallas_call x0 -> x1, Pallas kernels: none -> 52.2 us  [body(): pl.pallas_call(functools.partial(sum_kernel, dims), out_shape=jax.ShapeDt...]
    pallas_call x1, Pallas kernels: 11.5 us -> 8.33 us  [body(): north, south, edges = halo(back, back_left, back_right)]
    unnamed x54 -> x47, local copies, waits for them, and re-layouts: 15.3 us -> 17.5 us
  transfers between devices with their start and end apart: 1 -> 1, of which waited for: 1 -> 1; matrix products, arithmetic and copies ran while one was open for 3% -> 10% of each run, Pallas kernels for 11% -> 69%
where the time goes in v2:
time: 170 us
  Pallas kernels  123 us (72%)
  local copies, waits for them, and re-layouts  24.4 us (14%)
  between operations  14.3 us (8%)
  other arithmetic  5.45 us (3%)
  waiting for transfers between devices  1.93 us (1%)
    pallas_call x1, Pallas kernels, body(): pl.pallas_call(functools.partial(sum_kernel, dims), out_shape=jax.ShapeDt...  52.2 us
    pallas_call x1, Pallas kernels, body(): pl.pallas_call(functools.partial(mixer_kernel, factor, columns), out_shap...  32.9 us
    unnamed x47, local copies, waits for them, and re-layouts  17.5 us
    pallas_call x1, Pallas kernels, body(): pl.pallas_call(functools.partial(back_kernel, columns), out_shape=tile, i...  12.8 us
    pallas_call x1, Pallas kernels, body(): north, south, edges = halo(two_in, left, right)  10.8 us
    pallas_call x1, Pallas kernels, body(): north, south, edges = halo(back, back_left, back_right)  8.33 us
    pallas_call x1, Pallas kernels, body(): pl.pallas_call(functools.partial(level_kernel, factor, slot), out_shape=(...  6.34 us
  transfers between devices with their start and end apart: 1, of which 1 were waited for; matrix products, arithmetic and copies ran while one was open for 10% of the time, Pallas kernels for 69%

profile of v2, /device:TPU:0, one launch (start us, length us, event | category | flops | bytes accessed | tf_op | source)
XLA Modules:
  0.0 169.5 jit_solution(15150225818577859620)
XLA Ops:
  7.2 1.1 copy.39
  8.3 0.1 pad.15
  8.5 0.7 copy.60
  9.2 1.1 copy.40
  10.3 0.1 pad.16
  10.4 0.7 copy.61
  11.2 0.1 copy.41
  11.3 0.1 pad.17
  11.4 0.7 copy.62
  12.2 0.1 copy.42
  12.3 0.1 pad.18
  12.4 0.7 copy.63
  13.1 0.8 reshape.83.listing
  13.9 0.7 copy.44.le
  14.7 1.0 copy.45.lr
  15.6 6.3 %level.1 = (bf16[300,384]{1,0:T(8,128)(2,1)}, bf16[300,384]{1,0:T(8,128)(2,1)}, bf16[16,300]{1,0:T(8,128)(2,1)}, bf16[16,300]{1,0:T(8,128)(2,1)}, f32[8,384]{1,0...) custom-call(bf16[300,384]{1,0:T(8,128)(2,1)} %bitcast.28, bf16[300,384]{1,0:T(8,128)(2,1)} %bitcast.37, ...), custom_call_target="tpu_custom_call" | custom-call | tf_op jit(solution)/shard_map/level/pallas_call | solution.py:404
  22.1 0.1 copy.46
  22.2 0.4 rev.3
  22.6 0.7 pad.10.weights
  23.3 0.7 pad.11.weights
  24.0 0.8 select_convert_fusion.turn
  24.8 1.3 copy.47.rw
  26.1 0.1 reshape.71
  26.2 0.1 reshape.72
  26.3 0.7 add_convert_fusion.flags
  26.9 10.8 %halo.2 = (bf16[300,384]{1,0:T(8,128)(2,1)}, bf16[300,384]{1,0:T(8,128)(2,1)}, bf16[6,16,300]{2,1,0:T(8,128)(2,1)}) custom-call(bf16[300,384]{1,0:T(8,128)(2,1)} %get-tuple-element.27.tile.own, bf16[16,300]{1,0:T(8,128)(2,1)} %get-tuple-element.28.left, bf16[16,300]{1,0:T(8,128)(2,1)} %get-tuple-element.29.right), custom_call_target="tpu_custom_call" | custom-call | tf_op jit(solution)/shard_map/halo/pallas_call | solution.py:431
  37.8 0.6 broadcast_select_fusion.1.place_north
  38.4 32.9 %mixer.1 = (bf16[300,384]{1,0:T(8,128)(2,1)}, bf16[300,384]{1,0:T(8,128)(2,1)}, bf16[16,300]{1,0:T(8,128)(2,1)}, bf16[16,300]{1,0:T(8,128)(2,1)}, bf16[1280,768]{1,0:T(8,128)(2,1)}) custom-call(s32[2]{0:T(128)} %add_convert_fusion.flags, bf16[300,384]{1,0:T(8,128)(2,1)} %get-tuple-element.27.tile.own, bf16[300,384]{1,0:T(8,128)(2,1)} %get-tuple-element.30.north, ...), custom_call_target="tpu_custom_call" | custom-call | tf_op jit(solution)/shard_map/mixer/pallas_call | solution.py:441
  71.3 52.2 %sum.1 = bf16[32,40,768]{2,1,0:T(8,128)(2,1)} custom-call(bf16[32,40,768]{2,1,0:T(8,128)(2,1)} %bitcast.32), custom_call_target="tpu_custom_call" | custom-call | tf_op jit(solution)/shard_map/sum/pallas_call | solution.py:461
  123.6 0.8 convert_bitcast_fusion.1
  124.4 1.6 fusion
  126.0 0.1 reshape.70
  126.1 0.7 copy.52
  126.8 0.7 copy.53
  127.6 0.7 copy.54
  128.3 0.7 pad.12.north_weights
  129.0 8.3 %halo.3 = (bf16[300,384]{1,0:T(8,128)(2,1)}, bf16[300,384]{1,0:T(8,128)(2,1)}, bf16[6,16,300]{2,1,0:T(8,128)(2,1)}) custom-call(bf16[300,384]{1,0:T(8,128)(2,1)} %get-tuple-element.36.tile.own, bf16[16,300]{1,0:T(8,128)(2,1)} %get-tuple-element.37.left, bf16[16,300]{1,0:T(8,128)(2,1)} %get-tuple-element.38.right), custom_call_target="tpu_custom_call" | custom-call | tf_op jit(solution)/shard_map/halo/pallas_call | solution.py:481
  137.3 12.8 %back.1 = bf16[300,384]{1,0:T(8,128)(2,1)} custom-call(s32[2]{0:T(128)} %add_convert_fusion.flags, bf16[300,384]{1,0:T(8,128)(2,1)} %get-tuple-element.36.tile.own, bf16[300,384]{1,0:T(8,128)(2,1)} %get-tuple-element.39.north, bf16[300,384]{1,0:T(8,128)(2,1)} %get-tuple-element.40.south, bf16[6,16,300]{2,1,0:T(8,128)(2,1)} %get-tuple-element.41.edges, ...), custom_call_target="tpu_custom_call" | custom-call | tf_op jit(solution)/shard_map/back/pallas_call | solution.py:483
  150.1 1.0 reshape.73
  151.1 0.7 copy.55
  151.9 0.6 reshape.81
  152.5 0.8 copy.58
  153.3 0.8 copy.59
  154.2 1.2 convert_element_type.27
  155.4 1.2 convert_bitcast_fusion
  156.6 1.9 %all-reduce.6.cloned.1.call-done = (f32[4,75,300]{2,1,0:T(8,128)}, f32[4,300,75]{2,1,0:T(8,128)}) async-done(((f32[4,75,300]{2,1,0:T(8,128)}, f32[4,300,75]{2,1,0:T(8,128)}), (f32[4,75,300]{2,1,0:T(8,128)}, f32[4,300,75]{2,1,0:T(8,128)})) %all-reduce.6.cloned.1.call-update) | async-done | bytes 720016 | tf_op jit(solution)/shard_map/psum | solution.py:420
  158.6 2.0 %copy.56 = f32[4,75,300]{2,0,1:T(4,128)} copy(f32[4,75,300]{2,1,0:T(8,128)} %get-tuple-element.63) | data formatting | bytes 720000
  160.5 2.1 %copy.57 = f32[4,300,75]{1,0,2:T(4,128)} copy(f32[4,300,75]{2,1,0:T(8,128)} %get-tuple-element.64) | data formatting | bytes 720000
  (29 shorter events, 0.2 us)
Async XLA Ops:
  7.2 4.0 %copy-start.4 = (bf16[300,3,128]{2,0,1:T(8,128)(2,1)S(1)}, bf16[300,3,128]{2,0,1:T(8,128)(2,1)}, u32[]{:S(2)}) copy-start(bf16[300,3,128]{2,0,1:T(8,128)(2,1)} %param.16) | copy-start | bytes 691204
  7.2 151.4 %all-reduce.6.cloned.1.call-start = ((), (), s32[]{:S(2)}) async-start(), calls=%async_computation | async-start | bytes 2228224 | tf_op jit(solution)/shard_map/psum | solution.py:420
  8.5 3.7 %copy-start.5 = (bf16[300,3,128]{2,0,1:T(8,128)(2,1)S(1)}, bf16[300,3,128]{2,0,1:T(8,128)(2,1)}, u32[]{:S(2)}) copy-start(bf16[300,3,128]{2,0,1:T(8,128)(2,1)} %param.17) | copy-start | bytes 691204
  10.4 2.7 %copy-start.11 = (s32[1,1,8,48]{3,2,1,0:T(8,128)S(1)}, s32[1,1,8,48]{3,2,1,0:T(8,128)}, u32[]{:S(2)}) copy-start(s32[1,1,8,48]{3,2,1,0:T(8,128)} %param.18) | copy-start | bytes 4612
  10.4 3.5 %copy-start.7 = (bf16[4,75,300]{2,0,1:T(4,128)(2,1)S(1)}, bf16[4,75,300]{2,0,1:T(4,128)(2,1)}, u32[]{:S(2)}) copy-start(bf16[4,75,300]{2,0,1:T(4,128)(2,1)} %param.22) | copy-start | bytes 540004
  11.2 3.5 %copy-start.8 = (bf16[4,300,75]{1,0,2:T(4,128)(2,1)S(1)}, bf16[4,300,75]{1,0,2:T(4,128)(2,1)}, u32[]{:S(2)}) copy-start(bf16[4,300,75]{1,0,2:T(4,128)(2,1)} %param.23) | copy-start | bytes 540004
  13.9 8.1 %copy-start.9 = (bf16[300,7,7]{0,2,1:T(8,128)(2,1)S(1)}, bf16[300,7,7]{0,2,1:T(8,128)(2,1)}, u32[]{:S(2)}) copy-start(bf16[300,7,7]{0,2,1:T(8,128)(2,1)} %param.19) | copy-start | bytes 88204
  22.0 2.9 %copy-start.2 = (bf16[1200,300]{0,1:T(8,128)(2,1)S(1)}, bf16[1200,300]{0,1:T(8,128)(2,1)}, u32[]{:S(2)}) copy-start(bf16[1200,300]{0,1:T(8,128)(2,1)} %param.21) | copy-start | bytes 2160004
  22.0 4.1 %copy-start = (bf16[300,384]{1,0:T(8,128)(2,1)S(1)}, bf16[300,384]{1,0:T(8,128)(2,1)}, u32[]{:S(2)}) copy-start(bf16[300,384]{1,0:T(8,128)(2,1)} %get-tuple-element.27.tile.own) | copy-start | bytes 691204
  22.2 4.0 %copy-start.1 = (bf16[300,384]{1,0:T(8,128)(2,1)S(1)}, bf16[300,384]{1,0:T(8,128)(2,1)}, u32[]{:S(2)}) copy-start(bf16[300,384]{1,0:T(8,128)(2,1)} %get-tuple-element.33.total) | copy-start | bytes 691204
  24.0 13.8 %copy-start.3 = (bf16[2,16,384]{2,1,0:T(8,128)(2,1)S(1)}, bf16[2,16,384]{2,1,0:T(8,128)(2,1)}, u32[]{:S(2)}) copy-start(bf16[2,16,384]{2,1,0:T(8,128)(2,1)} %constant.25.clone.place_mid.place_south) | copy-start | bytes 73732
  24.0 13.8 %copy-start.10 = (bf16[2,16,384]{2,1,0:T(8,128)(2,1)S(1)}, bf16[2,16,384]{2,1,0:T(8,128)(2,1)}, u32[]{:S(2)}) copy-start(bf16[2,16,384]{2,1,0:T(8,128)(2,1)} %constant.26.clone) | copy-start | bytes 73732
  123.5 2.5 %copy-start.6 = (bf16[300,384]{1,0:T(8,128)(2,1)S(1)}, bf16[300,384]{1,0:T(8,128)(2,1)}, u32[]{:S(2)}) copy-start(bf16[300,384]{1,0:T(8,128)(2,1)} %get-tuple-element.35) | copy-start | bytes 691204
Sparse Core Ops, SparseCore 0:
  22.1 136.3 all-reduce.5
